TPU v7x, 32 devices: a whole 2x2x4 slice. The times are simulated.
32 devices in a mesh: regroup: 2 (over y), loop: 4 (over z), replica: 4 (over x, core).
Axes of the slice: x: 2, y: 2, z: 4, core: 2. Of those that a mesh axis runs over, the one named last changes fastest.
Arguments:
- features: bfloat16 [4, 4, 1024, 256], P('replica', 'loop', None, 'regroup'), may hold values from -6 to 6
- weight: bfloat16 [256, 256], replicated, may hold values from -0.375 to 0.375
- tiles: bfloat16 [4, 4, 2, 32, 128, 128], P('replica', 'loop', 'regroup'), may hold values from 0 to 1, as said below
- tile_row: int32 [4, 4, 2, 32], P('replica', 'loop', 'regroup'), may hold values from 0 to 3, as said below
- tile_col: int32 [4, 4, 2, 32], P('replica', 'loop', 'regroup'), may hold values from 0 to 3, as said below
- tile_width: int32 [4, 4, 2, 32], P('replica', 'loop', 'regroup'), may hold values from 0 to 128, as said below
- cotangent: bfloat16 [4, 4, 2, 512, 256], P('replica', 'loop', 'regroup'), may hold values from -6 to 6
Outputs:
- output: bfloat16 [4, 4, 2, 512, 256], P('replica', 'loop', 'regroup')
- grad_feat: bfloat16 [4, 4, 1024, 256], P('replica', 'loop', None, 'regroup')
- grad_weight: float32 [256, 256], replicated
Inputs may be any that keep to these rules, and one draw needn't show every extreme that they name: `tiles`: entries are 0 or between 0.25 and 1. `tile_row`: slot k < 4 of every device names cell block k. tile_col[r, l, g, s] is l - 1, l or l + 1 modulo 4. `tile_width`: each device's live slots come first, from 4 to 32 of them; some device has exactly 4 live and some all 32; slot 0 is live with width 128.
All inputs are finite; a program needn't handle non-finite values.
Results may differ from a plain program's by a relative error of at most 0.013.
Values may be sent and summed in bfloat16 or wider, within the bound.
A program may use at most 64 MiB of HBM per device.

v0:
```python
import math
import jax
import jax.numpy as jnp
from jax import lax
from jax.sharding import PartitionSpec as P

EPSILON = 1e-06


def shifted(block, axis, distance):
    devices = range(lax.axis_size(axis))
    route = [((i - distance) % len(devices), i) for i in devices]
    return lax.ppermute(block, axis, route)


def rms_scale(values):
    return values * lax.rsqrt(jnp.mean(values * values, axis=-1, keepdims=True) + EPSILON)


def per_device(features, weight, tiles, tile_row, tile_col, tile_width, cotangent):
    cell_rows = lax.all_to_all(features, "regroup", split_axis=2, concat_axis=3, tiled=True)[0, 0]
    cells, width = cell_rows.shape
    edge = tiles.shape[-1]
    blocks = cells // edge
    loops = lax.axis_size("loop")
    high = lax.Precision.HIGHEST
    rows_idx = tile_row[0, 0, 0]
    cols_idx = tile_col[0, 0, 0]
    widths = tile_width[0, 0, 0]
    column = jnp.arange(edge, dtype=jnp.int32)
    live_tiles = jnp.where(
        column[None, None, :] < widths[:, None, None], tiles[0, 0, 0], jnp.zeros((), tiles.dtype)
    )
    row_hot = (rows_idx[:, None] == jnp.arange(blocks, dtype=jnp.int32)[None, :]).astype(
        jnp.float32
    )
    row_sums = jnp.sum(live_tiles, axis=2, dtype=jnp.float32)
    cell_deg = 1.0 + jnp.einsum("tr,ti->ri", row_hot, row_sums, precision=high).reshape(cells)
    cell_root = jnp.sqrt(cell_deg)[:, None]
    col_tile_sums = jnp.sum(live_tiles, axis=1, dtype=jnp.float32)

    def to_nets(values, hot):
        gathered = values.reshape(blocks, edge, width)[rows_idx]
        per_tile = jnp.einsum(
            "tij,tif->tjf", live_tiles, gathered, preferred_element_type=jnp.float32
        )
        return jnp.einsum("tc,tjf->cjf", hot, per_tile, precision=high)

    def from_nets(blocked, index):
        gathered = blocked[index]
        per_tile = jnp.einsum(
            "tij,tjf->tif", live_tiles, gathered, preferred_element_type=jnp.float32
        )
        return jnp.einsum("tr,tif->rif", row_hot, per_tile, precision=high).reshape(cells, width)

    mixed = jnp.dot(cell_rows, weight, preferred_element_type=jnp.float32).astype(jnp.bfloat16)
    scaled = (mixed.astype(jnp.float32) / cell_root).astype(jnp.bfloat16)
    place = (cols_idx - lax.axis_index("loop") + loops) % loops
    net_index = jnp.where(place == 0, 1, jnp.where(place == 1, 2, 0)).astype(jnp.int32)
    near_hot = (net_index[:, None] == jnp.arange(3, dtype=jnp.int32)[None, :]).astype(jnp.float32)
    near_terms = to_nets(scaled, near_hot).astype(jnp.bfloat16)
    near_degs = jnp.einsum("tc,tj->cj", near_hot, col_tile_sums, precision=high).astype(
        jnp.bfloat16
    )
    below = shifted((near_terms[2], near_degs[2]), "loop", 1)
    above = shifted((near_terms[0], near_degs[0]), "loop", -1)
    totals = (
        near_terms[1].astype(jnp.float32)
        + below[0].astype(jnp.float32)
        + above[0].astype(jnp.float32)
    )
    degrees = (
        near_degs[1].astype(jnp.float32)
        + below[1].astype(jnp.float32)
        + above[1].astype(jnp.float32)
    )
    net_deg = (1.0 + degrees)[:, None]
    own_feat = (totals / net_deg).astype(jnp.bfloat16)
    prev_feat = shifted(own_feat, "loop", 1)
    next_feat = shifted(own_feat, "loop", -1)
    net_feat = jnp.stack([prev_feat, own_feat, next_feat])
    gathered_z = from_nets(net_feat, net_index) / cell_root
    normed, norm_back = jax.vjp(rms_scale, gathered_z)
    before = mixed.astype(jnp.float32) + normed
    output = jax.nn.silu(before).astype(jnp.bfloat16)
    sigmoid_v = jax.nn.sigmoid(before)
    grad_before = (
        cotangent[0, 0, 0].astype(jnp.float32) * sigmoid_v * (1.0 + before * (1.0 - sigmoid_v))
    )
    grad_z = norm_back(grad_before)[0]
    grad_scaled = (grad_z / cell_root).astype(jnp.bfloat16)
    grad_near = to_nets(grad_scaled, near_hot).astype(jnp.bfloat16)
    grad_below = shifted(grad_near[2], "loop", 1)
    grad_above = shifted(grad_near[0], "loop", -1)
    grad_sum_own = (
        grad_near[1].astype(jnp.float32)
        + grad_below.astype(jnp.float32)
        + grad_above.astype(jnp.float32)
    )
    grad_own = (grad_sum_own / net_deg).astype(jnp.bfloat16)
    grad_prev = shifted(grad_own, "loop", 1)
    grad_next = shifted(grad_own, "loop", -1)
    grad_net = jnp.stack([grad_prev, grad_own, grad_next])
    grad_mixed = (grad_before + from_nets(grad_net, net_index) / cell_root).astype(jnp.bfloat16)
    grad_rows = jnp.einsum(
        "cg,fg->cf", grad_mixed, weight, preferred_element_type=jnp.float32
    ).astype(jnp.bfloat16)
    grad_feat = lax.all_to_all(
        grad_rows[None, None], "regroup", split_axis=3, concat_axis=2, tiled=True
    )
    weight_term = jnp.einsum("cf,cg->fg", cell_rows, grad_mixed, preferred_element_type=jnp.float32)
    weight_part = lax.psum_scatter(
        weight_term, ("regroup", "loop"), scatter_dimension=0, tiled=True
    )
    weight_part = lax.psum(weight_part, "replica")
    weight_sum = lax.all_gather(weight_part, ("regroup", "loop"), axis=0, tiled=True)
    total_cells = cells * lax.axis_size("regroup") * loops * lax.axis_size("replica")
    grad_weight = weight_sum * (1.0 / math.sqrt(total_cells))
    return (output[None, None, None], grad_feat, grad_weight)


def solution(mesh):
    return jax.shard_map(
        per_device,
        mesh=mesh,
        in_specs=(
            P("replica", "loop", None, "regroup"),
            P(),
            P("replica", "loop", "regroup", None, None, None),
            P("replica", "loop", "regroup", None),
            P("replica", "loop", "regroup", None),
            P("replica", "loop", "regroup", None),
            P("replica", "loop", "regroup", None, None),
        ),
        out_specs=(
            P("replica", "loop", "regroup", None, None),
            P("replica", "loop", None, "regroup"),
            P(),
        ),
        check_vma=False,
    )
```

profile of v0, /device:TPU:0, one launch (start us, length us, event | category | flops | bytes accessed | tf_op | source)
XLA Modules:
  0.0 198.6 jit_solution(6420533877653232573)
XLA Ops:
  11.0 3.0 %collective-permute-start.2 = (bf16[128]{0:T(256)(128)(2,1)}, bf16[128]{0:T(256)(128)(2,1)}, u32[]{:S(2)}, u32[]{:S(2)}) collective-permute-start(bf16[128]{0:T(256)(128)(2,1)} %get-tuple-element.22), channel_id=1, source_target_pairs={{12,0},{0,4},{4,8},{8,12},{13,1},{1,5},{5,9},{9,13},{14,2},{2,6},{... | collective-permute-start | bytes 776 | tf_op jit(solution)/shard_map/ppermute | solution.py:13
  14.0 2.0 %collective-permute-start.3 = (bf16[128]{0:T(256)(128)(2,1)}, bf16[128]{0:T(256)(128)(2,1)}, u32[]{:S(2)}, u32[]{:S(2)}) collective-permute-start(bf16[128]{0:T(256)(128)(2,1)} %get-tuple-element.23), channel_id=1, source_target_pairs={{4,0},{8,4},{12,8},{0,12},{5,1},{9,5},{13,9},{1,13},{6,2},{10,6},{... | collective-permute-start | bytes 776 | tf_op jit(solution)/shard_map/ppermute | solution.py:13
  17.9 2.3 %reduce.1 = bf16[1024,128]{1,0:T(8,128)(2,1)S(1)} reduce(bf16[1024,1,1,128]{3,2,1,0:T(2,128)(2,1)S(1)} %bitcast.136, bf16[]{:T(256)} %broadcast.232), dimensions={1,2}, to_apply=%bitcast.131.reduce_sub_computation | reduce | bytes 524290
  20.9 3.4 %all-to-all-start = ((bf16[2,2,32768]{2,1,0:T(2,128)(2,1)}), bf16[2,2,32768]{2,1,0:T(2,128)(2,1)S(1)}, u32[]{:S(2)}, u32[]{:S(2)}) async-start(bf16[2,2,32768]{2,1,0:T(2,128)(2,1)} %reshape.232), calls=%async_computation | async-start | bytes 524288 | tf_op jit(solution)/shard_map/all_to_all | solution.py:21
  25.9 3.6 %all-to-all-done = bf16[2,2,32768]{2,1,0:T(2,128)(2,1)S(1)} async-done(((bf16[2,2,32768]{2,1,0:T(2,128)(2,1)}), bf16[2,2,32768]{2,1,0:T(2,128)(2,1)S(1)}, u32[]{:S(2)}, u32[]{:S(2)}) %all-to-all-start) | async-done | bytes 262176 | tf_op jit(solution)/shard_map/all_to_all | solution.py:21
  33.1 3.8 %fusion.9 = bf16[3,128,256]{2,0,1:T(4,128)(2,1)S(1)} fusion(f32[32,128,256]{2,1,0:T(8,128)S(1)} %fusion.23, s32[32]{0:T(128)S(1)} %copy-done.10), kind=kOutput, calls=%fused_computation.17 | convolution fusion | flops 37847136 | bytes 4391040 | tf_op jit(solution)/shard_map/tc,tjf->cjf/dot_general | solution.py:47
  37.3 2.1 %collective-permute-start.1 = (bf16[128,256]{1,0:T(8,128)(2,1)S(1)}, bf16[128,256]{1,0:T(8,128)(2,1)S(1)}, u32[]{:S(2)}, u32[]{:S(2)}) collective-permute-start(bf16[128,256]{1,0:T(8,128)(2,1)S(1)} %bitcast.146), channel_id=1, source_target_pairs={{4,0},{8,4},{12,8},{0,12},{5,1},{9,5},{13,9},{1,13},{6,2},{10,6},{... | collective-permute-start | bytes 196616 | tf_op jit(solution)/shard_map/ppermute | solution.py:13
  41.6 3.8 %collective-permute-done = bf16[128,256]{1,0:T(8,128)(2,1)S(1)} collective-permute-done((bf16[128,256]{1,0:T(8,128)(2,1)S(1)}, bf16[128,256]{1,0:T(8,128)(2,1)S(1)}, u32[]{:S(2)}, u32[]{:S(2)}) %collective-permute-start) | collective-permute-done | bytes 65568 | tf_op jit(solution)/shard_map/ppermute | solution.py:13
  45.6 2.0 %collective-permute-start.4 = (bf16[128,256]{1,0:T(8,128)(2,1)S(1)}, bf16[128,256]{1,0:T(8,128)(2,1)S(1)}, u32[]{:S(2)}, u32[]{:S(2)}) collective-permute-start(bf16[128,256]{1,0:T(8,128)(2,1)S(1)} %fusion.27), channel_id=1, source_target_pairs={{12,0},{0,4},{4,8},{8,12},{13,1},{1,5},{5,9},{9,13},{14,2},{2,6},{... | collective-permute-start | bytes 196616 | tf_op jit(solution)/shard_map/ppermute | solution.py:13
  47.6 2.2 %collective-permute-done.5 = bf16[128,256]{1,0:T(8,128)(2,1)S(1)} collective-permute-done((bf16[128,256]{1,0:T(8,128)(2,1)S(1)}, bf16[128,256]{1,0:T(8,128)(2,1)S(1)}, u32[]{:S(2)}, u32[]{:S(2)}) %collective-permute-start.5) | collective-permute-done | bytes 65568 | tf_op jit(solution)/shard_map/ppermute | solution.py:13
  49.8 2.0 %collective-permute-done.4 = bf16[128,256]{1,0:T(8,128)(2,1)S(1)} collective-permute-done((bf16[128,256]{1,0:T(8,128)(2,1)S(1)}, bf16[128,256]{1,0:T(8,128)(2,1)S(1)}, u32[]{:S(2)}, u32[]{:S(2)}) %collective-permute-start.4) | collective-permute-done | bytes 65568 | tf_op jit(solution)/shard_map/ppermute | solution.py:13
  53.5 4.0 %fusion.19 = (f32[4,128]{0,1:T(8,128)S(1)}, f32[4,128,256]{2,0,1:T(4,128)S(1)}) fusion(f32[4,128]{0,1:T(8,128)S(1)} %copy-done.8, f32[32,128,256]{2,1,0:T(8,128)S(1)} %fusion.22, s32[32]{0:T(128)S(1)} %bitcast.156), kind=kOutput, calls=%fused_computation.39 | convolution fusion | flops 50724480 | bytes 4722816 | tf_op jit(solution)/shard_map/tr,tif->rif/dot_general | solution.py:54
  61.1 3.8 %fusion.2 = bf16[3,128,256]{2,0,1:T(4,128)(2,1)S(1)} fusion(f32[32,128,256]{2,1,0:T(8,128)S(1)} %fusion.21, s32[32]{0:T(128)S(1)} %copy-done.11), kind=kOutput, calls=%fused_computation.6 | convolution fusion | flops 37748832 | bytes 4391040 | tf_op jit(solution)/shard_map/tc,tjf->cjf/dot_general | solution.py:47
  65.0 3.8 %collective-permute-start.7 = (bf16[128,256]{1,0:T(8,128)(2,1)S(1)}, bf16[128,256]{1,0:T(8,128)(2,1)S(1)}, u32[]{:S(2)}, u32[]{:S(2)}) collective-permute-start(bf16[128,256]{1,0:T(8,128)(2,1)S(1)} %get-tuple-element.21), channel_id=1, source_target_pairs={{4,0},{8,4},{12,8},{0,12},{5,1},{9,5},{13,9},{1,13},{6,2},{10,6},{... | collective-permute-start | bytes 196616 | tf_op jit(solution)/shard_map/ppermute | solution.py:13
  68.9 2.2 %collective-permute-done.6 = bf16[128,256]{1,0:T(8,128)(2,1)S(1)} collective-permute-done((bf16[128,256]{1,0:T(8,128)(2,1)S(1)}, bf16[128,256]{1,0:T(8,128)(2,1)S(1)}, u32[]{:S(2)}, u32[]{:S(2)}) %collective-permute-start.6) | collective-permute-done | bytes 65568 | tf_op jit(solution)/shard_map/ppermute | solution.py:13
  71.2 4.2 %collective-permute-start.9 = (bf16[128,256]{1,0:T(8,128)(2,1)S(1)}, bf16[128,256]{1,0:T(8,128)(2,1)S(1)}, u32[]{:S(2)}, u32[]{:S(2)}) collective-permute-start(bf16[128,256]{1,0:T(8,128)(2,1)S(1)} %fusion.30), channel_id=1, source_target_pairs={{4,0},{8,4},{12,8},{0,12},{5,1},{9,5},{13,9},{1,13},{6,2},{10,6},{... | collective-permute-start | bytes 196616 | tf_op jit(solution)/shard_map/ppermute | solution.py:13
  75.4 1.9 collective-permute-done.9
  77.3 4.2 %collective-permute-done.8 = bf16[128,256]{1,0:T(8,128)(2,1)S(1)} collective-permute-done((bf16[128,256]{1,0:T(8,128)(2,1)S(1)}, bf16[128,256]{1,0:T(8,128)(2,1)S(1)}, u32[]{:S(2)}, u32[]{:S(2)}) %collective-permute-start.8) | collective-permute-done | bytes 65568 | tf_op jit(solution)/shard_map/ppermute | solution.py:13
  82.9 3.8 %fusion = f32[4,128,256]{2,0,1:T(4,128)S(1)} fusion(f32[32,128,256]{2,1,0:T(8,128)S(1)} %fusion.20, s32[32]{0:T(128)S(1)} %bitcast.157), kind=kOutput, calls=%fused_computation.4 | convolution fusion | flops 50331776 | bytes 4718720 | tf_op jit(solution)/shard_map/tr,tif->rif/dot_general | solution.py:54
  89.5 2.2 %reduce.2 = bf16[256,512]{1,0:T(8,128)(2,1)S(1)} reduce(bf16[256,1,1,512]{3,2,1,0:T(2,128)(2,1)S(1)} %bitcast.137, bf16[]{:T(256)} %broadcast.232), dimensions={1,2}, to_apply=%bitcast.110.reduce_sub_computation | reduce | bytes 524290
  91.9 7.6 %all_to_all.33 = bf16[2,2,32768]{2,1,0:T(2,128)(2,1)S(1)} all-to-all(bf16[2,2,32768]{2,1,0:T(2,128)(2,1)S(1)} %reshape.234), channel_id=1, replica_groups=mesh['regroup'=2,'loop'=4,'replica'=4] {'regroup'}, dimensions={0} | all-to-all | bytes 524288 | tf_op jit(solution)/shard_map/all_to_all | solution.py:108
  100.6 46.8 %reduce-scatter.4.cloned.1.call-done = f32[32,256]{1,0:T(8,128)} async-done(((f32[256,256]{1,0:T(8,128)}), f32[32,256]{1,0:T(8,128)}) %reduce-scatter.4.cloned.1.call-update) | async-done | bytes 32784
  148.2 11.5 %psum.7 = f32[32,256]{0,1:T(8,128)S(1)} all-reduce(f32[32,256]{0,1:T(8,128)S(1)} %copy.103), channel_id=1, replica_groups=mesh['regroup'=2,'loop'=4,'replica'=4] {'replica'}, use_global_device_ids=true, to_apply=%region_5.6 | all-reduce | flops 8192 | bytes 65536 | tf_op jit(solution)/shard_map/psum | solution.py:115
  159.8 31.3 %all_gather.3 = f32[256,256]{1,0:T(8,128)S(1)} all-gather(f32[32,256]{1,0:T(8,128)S(1)} %copy.99), channel_id=1, replica_groups=mesh['regroup'=2,'loop'=4,'replica'=4] {'regroup','loop'}, dimensions={0}, use_global_device_ids=true | all-gather | bytes 294912 | tf_op jit(solution)/shard_map/all_gather | solution.py:116
  (104 shorter events, 26.5 us)
Async XLA Ops:
  7.2 22.9 %copy-start = (bf16[256,256]{1,0:T(8,128)(2,1)S(1)}, bf16[256,256]{1,0:T(8,128)(2,1)}, u32[]{:S(2)}) copy-start(bf16[256,256]{1,0:T(8,128)(2,1)} %param.8) | copy-start | bytes 393220
  7.2 17.3 %copy-start.18 = (s32[1,1,1,32]{3,2,1,0:T(1,128)S(1)}, s32[1,1,1,32]{3,2,1,0:T(1,128)}, u32[]{:S(2)}) copy-start(s32[1,1,1,32]{3,2,1,0:T(1,128)} %param.11) | copy-start | bytes 388
  7.2 17.8 %copy-start.14 = (s32[1,1,1,32]{3,2,1,0:T(1,128)S(1)}, s32[1,1,1,32]{3,2,1,0:T(1,128)}, u32[]{:S(2)}) copy-start(s32[1,1,1,32]{3,2,1,0:T(1,128)} %param.10) | copy-start | bytes 388
  8.6 16.4 %copy-start.9 = (s32[32]{0:T(128)}, s32[32]{0:T(128)S(1)}, u32[]{:S(2)}) copy-start(s32[32]{0:T(128)S(1)} %compare_select_fusion.8) | copy-start | bytes 388
  11.0 28.4 %collective-permute-start.2 = (bf16[128]{0:T(256)(128)(2,1)}, bf16[128]{0:T(256)(128)(2,1)}, u32[]{:S(2)}, u32[]{:S(2)}) collective-permute-start(bf16[128]{0:T(256)(128)(2,1)} %get-tuple-element.22), channel_id=1, source_target_pairs={{12,0},{0,4},{4,8},{8,12},{13,1},{1,5},{5,9},{9,13},{14,2},{2,6},{... | collective-permute-start | bytes 776 | tf_op jit(solution)/shard_map/ppermute | solution.py:13
  14.0 25.4 %collective-permute-start.3 = (bf16[128]{0:T(256)(128)(2,1)}, bf16[128]{0:T(256)(128)(2,1)}, u32[]{:S(2)}, u32[]{:S(2)}) collective-permute-start(bf16[128]{0:T(256)(128)(2,1)} %get-tuple-element.23), channel_id=1, source_target_pairs={{4,0},{8,4},{12,8},{0,12},{5,1},{9,5},{13,9},{1,13},{6,2},{10,6},{... | collective-permute-start | bytes 776 | tf_op jit(solution)/shard_map/ppermute | solution.py:13
  20.9 8.6 %all-to-all-start = ((bf16[2,2,32768]{2,1,0:T(2,128)(2,1)}), bf16[2,2,32768]{2,1,0:T(2,128)(2,1)S(1)}, u32[]{:S(2)}, u32[]{:S(2)}) async-start(bf16[2,2,32768]{2,1,0:T(2,128)(2,1)} %reshape.232), calls=%async_computation | async-start | bytes 524288 | tf_op jit(solution)/shard_map/all_to_all | solution.py:21
  24.4 123.0 %reduce-scatter.4.cloned.1.call-start = ((), (), s32[]{:S(2)}) async-start(), calls=%async_computation.3 | async-start | bytes 294912
  30.0 1.1 copy-start.4
  31.1 1.2 copy-start.1
  33.1 14.5 %copy-start.17 = (s32[32]{0:T(128)S(1)}, s32[32]{0:T(128)}, u32[]{:S(2)}) copy-start(s32[32]{0:T(128)} %fusion.43) | copy-start | bytes 388
  37.3 4.3 %collective-permute-start.1 = (bf16[128,256]{1,0:T(8,128)(2,1)S(1)}, bf16[128,256]{1,0:T(8,128)(2,1)S(1)}, u32[]{:S(2)}, u32[]{:S(2)}) collective-permute-start(bf16[128,256]{1,0:T(8,128)(2,1)S(1)} %bitcast.146), channel_id=1, source_target_pairs={{4,0},{8,4},{12,8},{0,12},{5,1},{9,5},{13,9},{1,13},{6,2},{10,6},{... | collective-permute-start | bytes 196616 | tf_op jit(solution)/shard_map/ppermute | solution.py:13
  39.4 6.1 %collective-permute-start = (bf16[128,256]{1,0:T(8,128)(2,1)S(1)}, bf16[128,256]{1,0:T(8,128)(2,1)S(1)}, u32[]{:S(2)}, u32[]{:S(2)}) collective-permute-start(bf16[128,256]{1,0:T(8,128)(2,1)S(1)} %bitcast.145), channel_id=1, source_target_pairs={{12,0},{0,4},{4,8},{8,12},{13,1},{1,5},{5,9},{9,13},{14,2},{2,6},{... | collective-permute-start | bytes 196616 | tf_op jit(solution)/shard_map/ppermute | solution.py:13
  40.0 11.9 %copy-start.12 = (f32[128]{0:T(128)}, f32[128]{0:T(128)S(1)}, u32[]{:S(2)}) copy-start(f32[128]{0:T(128)S(1)} %fusion.48) | copy-start | bytes 1540
  45.5 4.3 %collective-permute-start.5 = (bf16[128,256]{1,0:T(8,128)(2,1)S(1)}, bf16[128,256]{1,0:T(8,128)(2,1)S(1)}, u32[]{:S(2)}, u32[]{:S(2)}) collective-permute-start(bf16[128,256]{1,0:T(8,128)(2,1)S(1)} %fusion.27), channel_id=1, source_target_pairs={{4,0},{8,4},{12,8},{0,12},{5,1},{9,5},{13,9},{1,13},{6,2},{10,6},{... | collective-permute-start | bytes 196616 | tf_op jit(solution)/shard_map/ppermute | solution.py:13
  45.6 6.3 %collective-permute-start.4 = (bf16[128,256]{1,0:T(8,128)(2,1)S(1)}, bf16[128,256]{1,0:T(8,128)(2,1)S(1)}, u32[]{:S(2)}, u32[]{:S(2)}) collective-permute-start(bf16[128,256]{1,0:T(8,128)(2,1)S(1)} %fusion.27), channel_id=1, source_target_pairs={{12,0},{0,4},{4,8},{8,12},{13,1},{1,5},{5,9},{9,13},{14,2},{2,6},{... | collective-permute-start | bytes 196616 | tf_op jit(solution)/shard_map/ppermute | solution.py:13
  53.4 4.2 %copy-start.6 = (f32[512,256]{1,0:T(8,128)S(1)}, f32[512,256]{1,0:T(8,128)}, u32[]{:S(2)}) copy-start(f32[512,256]{1,0:T(8,128)} %get-tuple-element.25) | copy-start | bytes 1572868
  53.5 4.2 %copy-start.7 = (bf16[1,1,1,512,256]{4,3,2,1,0:T(8,128)(2,1)S(1)}, bf16[1,1,1,512,256]{4,3,2,1,0:T(8,128)(2,1)}, u32[]{:S(2)}) copy-start(bf16[1,1,1,512,256]{4,3,2,1,0:T(8,128)(2,1)} %param.13) | copy-start | bytes 786436
  61.1 10.0 %copy-start.13 = (f32[128]{0:T(128)S(1)}, f32[128]{0:T(128)}, u32[]{:S(2)}) copy-start(f32[128]{0:T(128)} %copy-done.12) | copy-start | bytes 1540
  65.0 6.1 %collective-permute-start.6 = (bf16[128,256]{1,0:T(8,128)(2,1)S(1)}, bf16[128,256]{1,0:T(8,128)(2,1)S(1)}, u32[]{:S(2)}, u32[]{:S(2)}) collective-permute-start(bf16[128,256]{1,0:T(8,128)(2,1)S(1)} %get-tuple-element.20), channel_id=1, source_target_pairs={{12,0},{0,4},{4,8},{8,12},{13,1},{1,5},{5,9},{9,13},{14,2},{2,6},{... | collective-permute-start | bytes 196616 | tf_op jit(solution)/shard_map/ppermute | solution.py:13
  65.0 6.1 %collective-permute-start.7 = (bf16[128,256]{1,0:T(8,128)(2,1)S(1)}, bf16[128,256]{1,0:T(8,128)(2,1)S(1)}, u32[]{:S(2)}, u32[]{:S(2)}) collective-permute-start(bf16[128,256]{1,0:T(8,128)(2,1)S(1)} %get-tuple-element.21), channel_id=1, source_target_pairs={{4,0},{8,4},{12,8},{0,12},{5,1},{9,5},{13,9},{1,13},{6,2},{10,6},{... | collective-permute-start | bytes 196616 | tf_op jit(solution)/shard_map/ppermute | solution.py:13
  71.2 6.1 %collective-permute-start.9 = (bf16[128,256]{1,0:T(8,128)(2,1)S(1)}, bf16[128,256]{1,0:T(8,128)(2,1)S(1)}, u32[]{:S(2)}, u32[]{:S(2)}) collective-permute-start(bf16[128,256]{1,0:T(8,128)(2,1)S(1)} %fusion.30), channel_id=1, source_target_pairs={{4,0},{8,4},{12,8},{0,12},{5,1},{9,5},{13,9},{1,13},{6,2},{10,6},{... | collective-permute-start | bytes 196616 | tf_op jit(solution)/shard_map/ppermute | solution.py:13
  75.4 6.1 %collective-permute-start.8 = (bf16[128,256]{1,0:T(8,128)(2,1)S(1)}, bf16[128,256]{1,0:T(8,128)(2,1)S(1)}, u32[]{:S(2)}, u32[]{:S(2)}) collective-permute-start(bf16[128,256]{1,0:T(8,128)(2,1)S(1)} %fusion.30), channel_id=1, source_target_pairs={{12,0},{0,4},{4,8},{8,12},{13,1},{1,5},{5,9},{9,13},{14,2},{2,6},{... | collective-permute-start | bytes 196616 | tf_op jit(solution)/shard_map/ppermute | solution.py:13
  82.9 3.9 %copy-start.3 = (f32[512,256]{1,0:T(8,128)S(1)}, f32[512,256]{1,0:T(8,128)}, u32[]{:S(2)}) copy-start(f32[512,256]{1,0:T(8,128)} %copy-done.2) | copy-start | bytes 1572868
  (7 other events, 5.7 us)
Sparse Core Ops, SparseCore 0:
  88.9 58.4 reduce-scatter.3
where the time goes:
time: 199 us
  waiting for transfers between devices  68.4 us (34%)
  blocking collectives  50.3 us (25%)
  starting transfers between devices  20.7 us (10%)
  matrix products  20.2 us (10%)
  between operations  14.5 us (7%)
  local copies, waits for them, and re-layouts  12.9 us (6%)
  other arithmetic  11.6 us (6%)
    unnamed x2, waiting for transfers between devices  46.8 us
    all_gather x1, blocking collectives, per_device(): lax.all_gather(weight_part, ('regroup', 'loop'), axis=0, tiled=True)  31.3 us
    ppermute x10, waiting for transfers between devices, shifted(): return lax.ppermute(block, axis, route)  18 us
    ppermute x10, starting transfers between devices, shifted(): return lax.ppermute(block, axis, route)  17.2 us
    psum x1, blocking collectives, per_device(): weight_part = lax.psum(weight_part, 'replica')  11.5 us
    dot_general x2, matrix products, from_nets(): jnp.einsum('tr,tif->rif', row_hot, per_tile, precision=high)  7.83 us
    dot_general x2, matrix products, to_nets(): return jnp.einsum('tc,tjf->cjf', hot, per_tile, precision=high)  7.66 us
    all_to_all x1, blocking collectives, per_device(): lax.all_to_all(grad_rows[None, None], 'regroup', split_axis=3, concat_axi...  7.56 us
  transfers between devices with their start and end apart: 12, of which 9 were waited for; matrix products, arithmetic and copies ran while one was open for 9% of the time, Pallas kernels for 0%

commit v1 on v0

--- a/solution.py
+++ b/solution.py
@@ -5,6 +5,12 @@
 from jax.sharding import PartitionSpec as P
 
 EPSILON = 1e-06
+
+
+def trade_parts(x, axis, split, join):
+    shards = jnp.split(x, lax.axis_size(axis), axis=split)
+    incoming = lax.all_to_all(jnp.stack(shards), axis, 0, 0)
+    return jnp.concatenate(incoming, axis=join)
 
 
 def shifted(block, axis, distance):
@@ -18,7 +24,7 @@
 
 
 def per_device(features, weight, tiles, tile_row, tile_col, tile_width, cotangent):
-    cell_rows = lax.all_to_all(features, "regroup", split_axis=2, concat_axis=3, tiled=True)[0, 0]
+    cell_rows = trade_parts(features, "regroup", 2, 3)[0, 0]
     cells, width = cell_rows.shape
     edge = tiles.shape[-1]
     blocks = cells // edge

time: 199 us -> 187 us (0.940)
  other arithmetic: 11.6 us -> 7.46 us
  local copies, waits for them, and re-layouts: 12.9 us -> 9.39 us
  waiting for transfers between devices: 68.4 us -> 66.1 us
  starting transfers between devices: 20.7 us -> 18.7 us
    reduce_scatter x0 -> x1, waiting for transfers between devices: none -> 46.9 us  [per_device(): lax.psum_scatter(weight_term, ('regroup', 'loop'), scatter_dimension=0, t...]
    unnamed x2 -> x1, waiting for transfers between devices: 46.8 us -> 0.02 us
    unnamed x51 -> x49, local copies, waits for them, and re-layouts: 7.11 us -> 2.71 us
    all_to_all x1, waiting for transfers between devices: 3.61 us -> 0.01 us  [trade_parts(): incoming = lax.all_to_all(jnp.stack(shards), axis, 0, 0)]
    ppermute x10, starting transfers between devices: 17.2 us -> 14.5 us  [shifted(): return lax.ppermute(block, axis, route)]
    unnamed x2 -> x1, other arithmetic: 4.45 us -> 2.21 us
  transfers between devices with their start and end apart: 12 -> 12, of which waited for: 9 -> 9; matrix products, arithmetic and copies ran while one was open for 9% -> 8% of each run, Pallas kernels for 0% -> 0%
where the time goes in v1:
time: 187 us
  waiting for transfers between devices  66.1 us (35%)
  blocking collectives  49.5 us (26%)
  matrix products  20.9 us (11%)
  starting transfers between devices  18.7 us (10%)
  between operations  14.5 us (8%)
  local copies, waits for them, and re-layouts  9.39 us (5%)
  other arithmetic  7.46 us (4%)
    reduce_scatter x1, waiting for transfers between devices, per_device(): lax.psum_scatter(weight_term, ('regroup', 'loop'), scatter_dimension=0, t...  46.9 us
    all_gather x1, blocking collectives, per_device(): lax.all_gather(weight_part, ('regroup', 'loop'), axis=0, tiled=True)  31.1 us
    ppermute x10, waiting for transfers between devices, shifted(): return lax.ppermute(block, axis, route)  19.2 us
    ppermute x10, starting transfers between devices, shifted(): return lax.ppermute(block, axis, route)  14.5 us
    psum x1, blocking collectives, per_device(): weight_part = lax.psum(weight_part, 'replica')  10.8 us
    dot_general x2, matrix products, from_nets(): jnp.einsum('tr,tif->rif', row_hot, per_tile, precision=high)  7.81 us
    dot_general x2, matrix products, to_nets(): return jnp.einsum('tc,tjf->cjf', hot, per_tile, precision=high)  7.66 us
    all_to_all x1, blocking collectives, per_device(): lax.all_to_all(grad_rows[None, None], 'regroup', split_axis=3, concat_axi...  7.56 us
  transfers between devices with their start and end apart: 12, of which 9 were waited for; matrix products, arithmetic and copies ran while one was open for 8% of the time, Pallas kernels for 0%

profile of v1, /device:TPU:0, one launch (start us, length us, event | category | flops | bytes accessed | tf_op | source)
XLA Modules:
  0.0 186.5 jit_solution(3267168057996213915)
XLA Ops:
  9.3 4.2 %all-to-all-start = ((bf16[2,1,1,512,128]{3,4,2,1,0:T(8,128)(2,1)}), bf16[2,1,1,512,128]{3,4,2,1,0:T(8,128)(2,1)S(1)}, u32[]{:S(2)}, u32[]{:S(2)}) async-start(bf16[2,1,1,512,128]{3,4,2,1,0:T(8,128)(2,1)} %pad_maximum_fusion), calls=%async_computation | async-start | bytes 524288 | tf_op jit(solution)/shard_map/all_to_all | solution.py:12
  14.8 4.3 %collective-permute-start.3 = (bf16[128]{0:T(256)(128)(2,1)}, bf16[128]{0:T(256)(128)(2,1)}, u32[]{:S(2)}, u32[]{:S(2)}) collective-permute-start(bf16[128]{0:T(256)(128)(2,1)} %get-tuple-element.16), channel_id=1, source_target_pairs={{4,0},{8,4},{12,8},{0,12},{5,1},{9,5},{13,9},{1,13},{6,2},{10,6},{... | collective-permute-start | bytes 776 | tf_op jit(solution)/shard_map/ppermute | solution.py:19
  23.1 3.8 %fusion.9 = bf16[3,128,256]{2,0,1:T(4,128)(2,1)S(1)} fusion(f32[32,128,256]{2,1,0:T(8,128)S(1)} %fusion.23, s32[32]{0:T(128)S(1)} %copy-done.10), kind=kOutput, calls=%fused_computation.17 | convolution fusion | flops 37847136 | bytes 4391040 | tf_op jit(solution)/shard_map/tc,tjf->cjf/dot_general | solution.py:53
  27.3 3.9 %collective-permute-start.1 = (bf16[128,256]{1,0:T(8,128)(2,1)S(1)}, bf16[128,256]{1,0:T(8,128)(2,1)S(1)}, u32[]{:S(2)}, u32[]{:S(2)}) collective-permute-start(bf16[128,256]{1,0:T(8,128)(2,1)S(1)} %bitcast.140), channel_id=1, source_target_pairs={{4,0},{8,4},{12,8},{0,12},{5,1},{9,5},{13,9},{1,13},{6,2},{10,6},{... | collective-permute-start | bytes 196616 | tf_op jit(solution)/shard_map/ppermute | solution.py:19
  31.9 1.1 collective-permute-done.1
  33.0 4.8 %collective-permute-done = bf16[128,256]{1,0:T(8,128)(2,1)S(1)} collective-permute-done((bf16[128,256]{1,0:T(8,128)(2,1)S(1)}, bf16[128,256]{1,0:T(8,128)(2,1)S(1)}, u32[]{:S(2)}, u32[]{:S(2)}) %collective-permute-start) | collective-permute-done | bytes 65568 | tf_op jit(solution)/shard_map/ppermute | solution.py:19
  38.0 2.0 %collective-permute-start.4 = (bf16[128,256]{1,0:T(8,128)(2,1)S(1)}, bf16[128,256]{1,0:T(8,128)(2,1)S(1)}, u32[]{:S(2)}, u32[]{:S(2)}) collective-permute-start(bf16[128,256]{1,0:T(8,128)(2,1)S(1)} %fusion.27), channel_id=1, source_target_pairs={{12,0},{0,4},{4,8},{8,12},{13,1},{1,5},{5,9},{9,13},{14,2},{2,6},{... | collective-permute-start | bytes 196616 | tf_op jit(solution)/shard_map/ppermute | solution.py:19
  40.0 2.2 %collective-permute-done.5 = bf16[128,256]{1,0:T(8,128)(2,1)S(1)} collective-permute-done((bf16[128,256]{1,0:T(8,128)(2,1)S(1)}, bf16[128,256]{1,0:T(8,128)(2,1)S(1)}, u32[]{:S(2)}, u32[]{:S(2)}) %collective-permute-start.5) | collective-permute-done | bytes 65568 | tf_op jit(solution)/shard_map/ppermute | solution.py:19
  42.3 2.0 %collective-permute-done.4 = bf16[128,256]{1,0:T(8,128)(2,1)S(1)} collective-permute-done((bf16[128,256]{1,0:T(8,128)(2,1)S(1)}, bf16[128,256]{1,0:T(8,128)(2,1)S(1)}, u32[]{:S(2)}, u32[]{:S(2)}) %collective-permute-start.4) | collective-permute-done | bytes 65568 | tf_op jit(solution)/shard_map/ppermute | solution.py:19
  45.9 4.0 %fusion.19 = (f32[4,128]{0,1:T(8,128)S(1)}, f32[4,128,256]{2,0,1:T(4,128)S(1)}) fusion(f32[4,128]{0,1:T(8,128)S(1)} %copy-done.8, f32[32,128,256]{2,1,0:T(8,128)S(1)} %fusion.22, s32[32]{0:T(128)S(1)} %bitcast.151), kind=kOutput, calls=%fused_computation.38 | convolution fusion | flops 50724480 | bytes 4722816 | tf_op jit(solution)/shard_map/tr,tif->rif/dot_general | solution.py:60
  50.1 1.1 multiply_reduce_fusion
  53.5 3.8 %fusion.2 = bf16[3,128,256]{2,0,1:T(4,128)(2,1)S(1)} fusion(f32[32,128,256]{2,1,0:T(8,128)S(1)} %fusion.21, s32[32]{0:T(128)S(1)} %copy-done.11), kind=kOutput, calls=%fused_computation.6 | convolution fusion | flops 37748832 | bytes 4391040 | tf_op jit(solution)/shard_map/tc,tjf->cjf/dot_general | solution.py:53
  57.5 2.0 %collective-permute-start.6 = (bf16[128,256]{1,0:T(8,128)(2,1)S(1)}, bf16[128,256]{1,0:T(8,128)(2,1)S(1)}, u32[]{:S(2)}, u32[]{:S(2)}) collective-permute-start(bf16[128,256]{1,0:T(8,128)(2,1)S(1)} %get-tuple-element.13), channel_id=1, source_target_pairs={{12,0},{0,4},{4,8},{8,12},{13,1},{1,5},{5,9},{9,13},{14,2},{2,6},{... | collective-permute-start | bytes 196616 | tf_op jit(solution)/shard_map/ppermute | solution.py:19
  59.5 2.6 %collective-permute-done.7 = bf16[128,256]{1,0:T(8,128)(2,1)S(1)} collective-permute-done((bf16[128,256]{1,0:T(8,128)(2,1)S(1)}, bf16[128,256]{1,0:T(8,128)(2,1)S(1)}, u32[]{:S(2)}, u32[]{:S(2)}) %collective-permute-start.7) | collective-permute-done | bytes 65568 | tf_op jit(solution)/shard_map/ppermute | solution.py:19
  62.1 1.7 collective-permute-done.6
  64.5 1.4 collective-permute-start.8
  66.0 2.2 %collective-permute-done.9 = bf16[128,256]{1,0:T(8,128)(2,1)S(1)} collective-permute-done((bf16[128,256]{1,0:T(8,128)(2,1)S(1)}, bf16[128,256]{1,0:T(8,128)(2,1)S(1)}, u32[]{:S(2)}, u32[]{:S(2)}) %collective-permute-start.9) | collective-permute-done | bytes 65568 | tf_op jit(solution)/shard_map/ppermute | solution.py:19
  68.2 2.4 %collective-permute-done.8 = bf16[128,256]{1,0:T(8,128)(2,1)S(1)} collective-permute-done((bf16[128,256]{1,0:T(8,128)(2,1)S(1)}, bf16[128,256]{1,0:T(8,128)(2,1)S(1)}, u32[]{:S(2)}, u32[]{:S(2)}) %collective-permute-start.8) | collective-permute-done | bytes 65568 | tf_op jit(solution)/shard_map/ppermute | solution.py:19
  72.1 3.8 %fusion = f32[4,128,256]{2,0,1:T(4,128)S(1)} fusion(f32[32,128,256]{2,1,0:T(8,128)S(1)} %fusion.20, s32[32]{0:T(128)S(1)} %bitcast.152), kind=kOutput, calls=%fused_computation.4 | convolution fusion | flops 50331776 | bytes 4718720 | tf_op jit(solution)/shard_map/tr,tif->rif/dot_general | solution.py:60
  79.0 2.2 %reduce.1 = bf16[256,512]{1,0:T(8,128)(2,1)S(1)} reduce(bf16[256,1,1,512]{3,2,1,0:T(2,128)(2,1)S(1)} %bitcast.131, bf16[]{:T(256)} %broadcast.232), dimensions={1,2}, to_apply=%bitcast.108.reduce_sub_computation | reduce | bytes 524290
  81.4 7.6 %all_to_all.23 = bf16[2,2,32768]{2,1,0:T(2,128)(2,1)S(1)} all-to-all(bf16[2,2,32768]{2,1,0:T(2,128)(2,1)S(1)} %reshape.233), channel_id=1, replica_groups=mesh['regroup'=2,'loop'=4,'replica'=4] {'regroup'}, dimensions={0} | all-to-all | bytes 524288 | tf_op jit(solution)/shard_map/all_to_all | solution.py:114
  90.2 46.9 %reduce-scatter.2.cloned.1.call-done = f32[32,256]{1,0:T(8,128)} async-done(((f32[256,256]{1,0:T(8,128)}), f32[32,256]{1,0:T(8,128)}) %reduce-scatter.2.cloned.1.call-update) | async-done | bytes 32784 | tf_op jit(solution)/shard_map/reduce_scatter | solution.py:118
  137.0 10.8 %psum.7 = f32[32,256]{1,0:T(8,128)S(1)} all-reduce(f32[32,256]{1,0:T(8,128)} %reduce-scatter.2.cloned.1.call-done), channel_id=1, replica_groups=mesh['regroup'=2,'loop'=4,'replica'=4] {'replica'}, use_global_device_ids=true, to_apply=%region_5.6 | all-reduce | flops 8192 | bytes 65536 | tf_op jit(solution)/shard_map/psum | solution.py:121
  147.8 31.1 %all_gather.3 = f32[256,256]{1,0:T(8,128)S(1)} all-gather(f32[32,256]{1,0:T(8,128)S(1)} %psum.7), channel_id=1, replica_groups=mesh['regroup'=2,'loop'=4,'replica'=4] {'regroup','loop'}, dimensions={0}, use_global_device_ids=true | all-gather | bytes 294912 | tf_op jit(solution)/shard_map/all_gather | solution.py:122
  (101 shorter events, 19.8 us)
Async XLA Ops:
  7.2 13.4 %copy-start = (bf16[256,256]{1,0:T(8,128)(2,1)S(1)}, bf16[256,256]{1,0:T(8,128)(2,1)}, u32[]{:S(2)}) copy-start(bf16[256,256]{1,0:T(8,128)(2,1)} %param.8) | copy-start | bytes 393220
  7.2 6.3 %copy-start.17 = (s32[1,1,1,32]{3,2,1,0:T(1,128)S(1)}, s32[1,1,1,32]{3,2,1,0:T(1,128)}, u32[]{:S(2)}) copy-start(s32[1,1,1,32]{3,2,1,0:T(1,128)} %param.12) | copy-start | bytes 388
  7.2 6.4 %copy-start.1 = (bf16[1,1,1,32,128,128]{5,4,3,2,1,0:T(8,128)(2,1)S(1)}, bf16[1,1,1,32,128,128]{5,4,3,2,1,0:T(8,128)(2,1)}, u32[]{:S(2)}) copy-start(bf16[1,1,1,32,128,128]{5,4,3,2,1,0:T(8,128)(2,1)} %param.9) | copy-start | bytes 3145732
  7.2 6.8 %copy-start.19 = (s32[1,1,1,32]{3,2,1,0:T(1,128)S(1)}, s32[1,1,1,32]{3,2,1,0:T(1,128)}, u32[]{:S(2)}) copy-start(s32[1,1,1,32]{3,2,1,0:T(1,128)} %param.11) | copy-start | bytes 388
  7.2 11.9 %copy-start.14 = (s32[1,1,1,32]{3,2,1,0:T(1,128)S(1)}, s32[1,1,1,32]{3,2,1,0:T(1,128)}, u32[]{:S(2)}) copy-start(s32[1,1,1,32]{3,2,1,0:T(1,128)} %param.10) | copy-start | bytes 388
  9.3 11.3 %all-to-all-start = ((bf16[2,1,1,512,128]{3,4,2,1,0:T(8,128)(2,1)}), bf16[2,1,1,512,128]{3,4,2,1,0:T(8,128)(2,1)S(1)}, u32[]{:S(2)}, u32[]{:S(2)}) async-start(bf16[2,1,1,512,128]{3,4,2,1,0:T(8,128)(2,1)} %pad_maximum_fusion), calls=%async_computation | async-start | bytes 524288 | tf_op jit(solution)/shard_map/all_to_all | solution.py:12
  13.5 123.5 %reduce-scatter.2.cloned.1.call-start = ((), (), s32[]{:S(2)}) async-start(), calls=%async_computation.3 | async-start | bytes 294912 | tf_op jit(solution)/shard_map/reduce_scatter | solution.py:118
  14.0 5.1 %copy-start.9 = (s32[32]{0:T(128)}, s32[32]{0:T(128)S(1)}, u32[]{:S(2)}) copy-start(s32[32]{0:T(128)S(1)} %compare_select_fusion.8) | copy-start | bytes 388
  14.8 16.5 %collective-permute-start.3 = (bf16[128]{0:T(256)(128)(2,1)}, bf16[128]{0:T(256)(128)(2,1)}, u32[]{:S(2)}, u32[]{:S(2)}) collective-permute-start(bf16[128]{0:T(256)(128)(2,1)} %get-tuple-element.16), channel_id=1, source_target_pairs={{4,0},{8,4},{12,8},{0,12},{5,1},{9,5},{13,9},{1,13},{6,2},{10,6},{... | collective-permute-start | bytes 776 | tf_op jit(solution)/shard_map/ppermute | solution.py:19
  19.1 12.2 %collective-permute-start.2 = (bf16[128]{0:T(256)(128)(2,1)}, bf16[128]{0:T(256)(128)(2,1)}, u32[]{:S(2)}, u32[]{:S(2)}) collective-permute-start(bf16[128]{0:T(256)(128)(2,1)} %get-tuple-element.15), channel_id=1, source_target_pairs={{12,0},{0,4},{4,8},{8,12},{13,1},{1,5},{5,9},{9,13},{14,2},{2,6},{... | collective-permute-start | bytes 776 | tf_op jit(solution)/shard_map/ppermute | solution.py:19
  23.1 16.9 %copy-start.18 = (s32[32]{0:T(128)S(1)}, s32[32]{0:T(128)}, u32[]{:S(2)}) copy-start(s32[32]{0:T(128)} %fusion.43) | copy-start | bytes 388
  27.3 5.8 %collective-permute-start.1 = (bf16[128,256]{1,0:T(8,128)(2,1)S(1)}, bf16[128,256]{1,0:T(8,128)(2,1)S(1)}, u32[]{:S(2)}, u32[]{:S(2)}) collective-permute-start(bf16[128,256]{1,0:T(8,128)(2,1)S(1)} %bitcast.140), channel_id=1, source_target_pairs={{4,0},{8,4},{12,8},{0,12},{5,1},{9,5},{13,9},{1,13},{6,2},{10,6},{... | collective-permute-start | bytes 196616 | tf_op jit(solution)/shard_map/ppermute | solution.py:19
  31.2 6.7 %collective-permute-start = (bf16[128,256]{1,0:T(8,128)(2,1)S(1)}, bf16[128,256]{1,0:T(8,128)(2,1)S(1)}, u32[]{:S(2)}, u32[]{:S(2)}) collective-permute-start(bf16[128,256]{1,0:T(8,128)(2,1)S(1)} %bitcast.141), channel_id=1, source_target_pairs={{12,0},{0,4},{4,8},{8,12},{13,1},{1,5},{5,9},{9,13},{14,2},{2,6},{... | collective-permute-start | bytes 196616 | tf_op jit(solution)/shard_map/ppermute | solution.py:19
  31.9 12.4 %copy-start.12 = (f32[128]{0:T(128)}, f32[128]{0:T(128)S(1)}, u32[]{:S(2)}) copy-start(f32[128]{0:T(128)S(1)} %fusion.48) | copy-start | bytes 1540
  38.0 4.3 %collective-permute-start.5 = (bf16[128,256]{1,0:T(8,128)(2,1)S(1)}, bf16[128,256]{1,0:T(8,128)(2,1)S(1)}, u32[]{:S(2)}, u32[]{:S(2)}) collective-permute-start(bf16[128,256]{1,0:T(8,128)(2,1)S(1)} %fusion.27), channel_id=1, source_target_pairs={{4,0},{8,4},{12,8},{0,12},{5,1},{9,5},{13,9},{1,13},{6,2},{10,6},{... | collective-permute-start | bytes 196616 | tf_op jit(solution)/shard_map/ppermute | solution.py:19
  38.0 6.3 %collective-permute-start.4 = (bf16[128,256]{1,0:T(8,128)(2,1)S(1)}, bf16[128,256]{1,0:T(8,128)(2,1)S(1)}, u32[]{:S(2)}, u32[]{:S(2)}) collective-permute-start(bf16[128,256]{1,0:T(8,128)(2,1)S(1)} %fusion.27), channel_id=1, source_target_pairs={{12,0},{0,4},{4,8},{8,12},{13,1},{1,5},{5,9},{9,13},{14,2},{2,6},{... | collective-permute-start | bytes 196616 | tf_op jit(solution)/shard_map/ppermute | solution.py:19
  45.9 4.2 %copy-start.6 = (f32[512,256]{1,0:T(8,128)S(1)}, f32[512,256]{1,0:T(8,128)}, u32[]{:S(2)}) copy-start(f32[512,256]{1,0:T(8,128)} %get-tuple-element.18) | copy-start | bytes 1572868
  45.9 4.2 %copy-start.7 = (bf16[1,1,1,512,256]{4,3,2,1,0:T(8,128)(2,1)S(1)}, bf16[1,1,1,512,256]{4,3,2,1,0:T(8,128)(2,1)}, u32[]{:S(2)}) copy-start(bf16[1,1,1,512,256]{4,3,2,1,0:T(8,128)(2,1)} %param.13) | copy-start | bytes 786436
  53.5 10.3 %copy-start.13 = (f32[128]{0:T(128)S(1)}, f32[128]{0:T(128)}, u32[]{:S(2)}) copy-start(f32[128]{0:T(128)} %copy-done.12) | copy-start | bytes 1540
  57.4 4.7 %collective-permute-start.7 = (bf16[128,256]{1,0:T(8,128)(2,1)S(1)}, bf16[128,256]{1,0:T(8,128)(2,1)S(1)}, u32[]{:S(2)}, u32[]{:S(2)}) collective-permute-start(bf16[128,256]{1,0:T(8,128)(2,1)S(1)} %get-tuple-element.14), channel_id=1, source_target_pairs={{4,0},{8,4},{12,8},{0,12},{5,1},{9,5},{13,9},{1,13},{6,2},{10,6},{... | collective-permute-start | bytes 196616 | tf_op jit(solution)/shard_map/ppermute | solution.py:19
  57.5 6.3 %collective-permute-start.6 = (bf16[128,256]{1,0:T(8,128)(2,1)S(1)}, bf16[128,256]{1,0:T(8,128)(2,1)S(1)}, u32[]{:S(2)}, u32[]{:S(2)}) collective-permute-start(bf16[128,256]{1,0:T(8,128)(2,1)S(1)} %get-tuple-element.13), channel_id=1, source_target_pairs={{12,0},{0,4},{4,8},{8,12},{13,1},{1,5},{5,9},{9,13},{14,2},{2,6},{... | collective-permute-start | bytes 196616 | tf_op jit(solution)/shard_map/ppermute | solution.py:19
  63.9 4.3 %collective-permute-start.9 = (bf16[128,256]{1,0:T(8,128)(2,1)S(1)}, bf16[128,256]{1,0:T(8,128)(2,1)S(1)}, u32[]{:S(2)}, u32[]{:S(2)}) collective-permute-start(bf16[128,256]{1,0:T(8,128)(2,1)S(1)} %fusion.30), channel_id=1, source_target_pairs={{4,0},{8,4},{12,8},{0,12},{5,1},{9,5},{13,9},{1,13},{6,2},{10,6},{... | collective-permute-start | bytes 196616 | tf_op jit(solution)/shard_map/ppermute | solution.py:19
  64.5 6.1 %collective-permute-start.8 = (bf16[128,256]{1,0:T(8,128)(2,1)S(1)}, bf16[128,256]{1,0:T(8,128)(2,1)S(1)}, u32[]{:S(2)}, u32[]{:S(2)}) collective-permute-start(bf16[128,256]{1,0:T(8,128)(2,1)S(1)} %fusion.30), channel_id=1, source_target_pairs={{12,0},{0,4},{4,8},{8,12},{13,1},{1,5},{5,9},{9,13},{14,2},{2,6},{... | collective-permute-start | bytes 196616 | tf_op jit(solution)/shard_map/ppermute | solution.py:19
  72.0 3.9 %copy-start.3 = (f32[512,256]{1,0:T(8,128)S(1)}, f32[512,256]{1,0:T(8,128)}, u32[]{:S(2)}) copy-start(f32[512,256]{1,0:T(8,128)} %copy-done.2) | copy-start | bytes 1572868
  (8 other events, 6.8 us)
Sparse Core Ops, SparseCore 0:
  77.9 59.0 reduce-scatter.1
